TPU v7x, 256 devices: a whole 4x4x8 slice. The times are simulated.
256 devices in a mesh: seq: 128 (over x_lo, y, z, core), head: 2 (over x_hi).
Axes of the slice: x: 4 (x_hi: 2, x_lo: 2; x = x_hi * 2 + x_lo), y: 4, z: 8, core: 2. Of those that a mesh axis runs over, the one named last changes fastest.
Arguments:
- queries: bfloat16 [16384, 3072], P('seq', 'head'), may hold values from -6 to 6
- keys: bfloat16 [16384, 3072], P('seq', 'head'), may hold values from -6 to 6
- values: bfloat16 [16384, 3072], P('seq', 'head'), may hold values from -6 to 6
- cache_k: bfloat16 [2048, 3072], P('seq', 'head'), may hold values from -6 to 6
- cache_v: bfloat16 [2048, 3072], P('seq', 'head'), may hold values from -6 to 6
- sink_k: bfloat16 [8, 3072], P(None, 'head'), may hold values from -6 to 6
- sink_v: bfloat16 [8, 3072], P(None, 'head'), may hold values from -6 to 6
- suffix_lengths: int32 [32], replicated, may hold values from 1 to 1024, 16384 in all
- request_group: int32 [32], replicated, may hold values from 0 to 1
- w_out: bfloat16 [3072, 3072], P('head'), may hold values from -0.109375 to 0.109375
Outputs:
- projected: bfloat16 [3072, 16384], P('head', 'seq')
All inputs are finite; a program needn't handle non-finite values.
Results may differ from a plain program's by a relative error of at most 0.011.
Values may be sent and summed in bfloat16 or wider, within the bound.
No kernel may reach another device: no remote copies, remote signals or barrier semaphores. Data moves between devices by JAX's collectives and lax.ppermute only.
A program may use at most 128 MiB of HBM per device.

v0:
```python
import math
import jax
import jax.numpy as jnp
from jax import lax
from jax.sharding import PartitionSpec as P

HD = 96
W = 1024
SINKS = 4


def from_behind(array, axis, by):
    devices = lax.axis_size(axis)
    pairs = [(i, i + by) for i in range(devices) if 0 <= i + by < devices]
    return lax.ppermute(array, axis, pairs)


def describe(index, starts, lengths, groups):
    inside = (starts[None, :] <= index[:, None]) & (index[:, None] < (starts + lengths)[None, :])
    flag = inside.astype(jnp.int32)
    found = jnp.sum(flag, axis=1)
    request = jnp.sum(flag * jnp.arange(starts.shape[0], dtype=jnp.int32)[None, :], axis=1)
    request = jnp.where(found > 0, request, -1)
    offset = index - jnp.sum(flag * starts[None, :], axis=1)
    group = jnp.sum(flag * groups[None, :], axis=1)
    return (request, offset, group)


def shards(
    queries, keys, values, cache_k, cache_v, sink_k, sink_v, suffix_lengths, request_group, w_out
):
    rows, width = queries.shape
    heads = width // HD
    scale = 1.0 / math.sqrt(HD)
    device = lax.axis_index("seq")
    starts = jnp.cumsum(suffix_lengths) - suffix_lengths
    index = device * rows + jnp.arange(rows, dtype=jnp.int32)
    req_q, off_q, grp_q = describe(index, starts, suffix_lengths, request_group)
    q_three = queries.reshape(rows, heads, HD)

    def absorb(state, key_rows, value_rows, mask):
        top, den, acc = state
        count = key_rows.shape[0]
        k_three = key_rows.reshape(count, heads, HD)
        v_three = value_rows.reshape(count, heads, HD)
        score = (
            jnp.einsum("shd,khd->hsk", q_three, k_three, preferred_element_type=jnp.float32) * scale
        )
        score = jnp.where(mask[None], score, jnp.float32(-1e30))
        new_top = jnp.maximum(top, jnp.max(score, axis=2))
        factor = jnp.exp(top - new_top)
        prob = jnp.where(mask[None], jnp.exp(score - new_top[:, :, None]), jnp.float32(0.0))
        den = den * factor + jnp.sum(prob, axis=2)
        part = jnp.einsum(
            "hsk,khd->hsd", prob.astype(jnp.bfloat16), v_three, preferred_element_type=jnp.float32
        )
        acc = acc * factor[:, :, None] + part
        return (new_top, den, acc)

    def suffix_mask(near):
        req_k, off_k, grp_k = describe(near, starts, suffix_lengths, request_group)
        return (
            (req_k[None, :] == req_q[:, None])
            & (near[None, :] <= index[:, None])
            & (index[:, None] - near[None, :] < W)
            & (near[None, :] >= 0)
        )

    state = (
        jnp.full((heads, rows), -1e30, jnp.float32),
        jnp.zeros((heads, rows), jnp.float32),
        jnp.zeros((heads, rows, HD), jnp.float32),
    )
    sink_group = jnp.arange(sink_k.shape[0], dtype=jnp.int32) // SINKS
    state = absorb(state, sink_k, sink_v, grp_q[:, None] == sink_group[None, :])
    pieces = (
        lax.all_gather(cache_k, "seq", axis=0, tiled=True),
        lax.all_gather(cache_v, "seq", axis=0, tiled=True),
    )
    slot = jnp.arange(pieces[0].shape[0], dtype=jnp.int32)
    state = absorb(
        state,
        pieces[0],
        pieces[1],
        (grp_q[:, None] == (slot // W)[None, :]) & ((slot % W)[None, :] > off_q[:, None]),
    )
    state = absorb(state, keys, values, suffix_mask(index))
    reach = W // rows
    current = (keys, values)
    for step in range(1, reach + 1):
        current = from_behind((current[0], current[1]), "seq", 1)
        near = (device - step) * rows + jnp.arange(rows, dtype=jnp.int32)
        state = absorb(state, current[0], current[1], suffix_mask(near))
    top, den, acc = state
    attn = (acc / den[:, :, None]).transpose(1, 0, 2).reshape(rows, width).astype(jnp.bfloat16)
    return lax.psum_scatter(
        jnp.einsum("cd,sc->ds", w_out, attn, preferred_element_type=jnp.float32).astype(
            jnp.bfloat16
        ),
        "head",
        scatter_dimension=0,
        tiled=True,
    )


def solution(mesh):
    placed = (
        P("seq", "head"),
        P("seq", "head"),
        P("seq", "head"),
        P("seq", "head"),
        P("seq", "head"),
        P(None, "head"),
        P(None, "head"),
        P(),
        P(),
        P("head", None),
    )
    return jax.shard_map(
        shards, mesh=mesh, in_specs=placed, out_specs=P("head", "seq"), check_vma=False
    )
```

profile of v0, /device:TPU:1, one launch (start us, length us, event | category | flops | bytes accessed | tf_op | source)
XLA Modules:
  0.0 552.5 jit_solution(7046040993679264815)
XLA Ops:
  8.1 4.9 collective-permute-start
  13.0 1.9 collective-permute-start.1
  16.6 0.8 convert_reduce_fusion
  17.6 1.1 fusion.98
  18.7 3.9 collective-permute-start.2
  22.7 3.8 collective-permute-start.3
  26.5 1.2 copy.90
  27.7 0.8 reshape.1639
  28.6 1.4 fusion.171
  30.0 2.6 collective-permute-start.4
  33.2 4.4 collective-permute-start.5
  37.6 1.2 copy.95
  38.8 1.9 copy.96
  40.7 1.4 reshape.1640
  42.2 1.0 fusion.170
  43.1 1.9 collective-permute-start.6
  45.1 3.9 collective-permute-start.7
  49.0 1.0 compare_and_fusion
  50.0 0.9 collective-permute-done.6
  50.9 4.4 collective-permute-start.8
  55.3 4.3 collective-permute-start.9
  60.7 1.0 copy.99
  61.7 1.0 fusion.169
  62.6 1.9 copy.101
  64.5 2.3 collective-permute-start.10
  66.9 4.4 collective-permute-start.11
  71.3 2.0 fusion.168
  73.3 1.9 copy.102
  75.2 1.9 copy.104
  77.1 1.9 copy.105
  79.0 3.0 fusion.167
  82.0 1.9 copy.107
  83.9 2.9 collective-permute-start.12
  86.8 4.4 collective-permute-start.13
  91.2 2.9 fusion.166
  94.1 1.9 copy.108
  96.0 1.9 copy.110
  97.9 1.9 copy.111
  99.9 2.9 fusion.165
  102.8 1.9 copy.113
  104.7 3.3 collective-permute-start.14
  108.0 4.7 collective-permute-start.15
  112.7 3.0 fusion.164
  115.7 1.9 copy.114
  117.6 1.9 copy.116
  119.5 1.9 copy.117
  121.5 2.9 fusion.163
  124.4 1.9 copy.119
  126.3 1.9 copy.120
  128.2 3.0 fusion.162
  131.2 144.8 %all-gather.3.cloned.1.call-done = bf16[2048,1536]{1,0:T(8,128)(2,1)} async-done(((bf16[16,1536]{1,0:T(8,128)(2,1)}), bf16[2048,1536]{1,0:T(8,128)(2,1)}) %all-gather.3.cloned.1.call-update) | async-done | bytes 6291472 | tf_op jit(solution)/shard_map/all_gather | solution.py:77
  276.0 8.7 %copy.93 = bf16[2048,1536]{0,1:T(8,128)(2,1)} copy(bf16[2048,1536]{1,0:T(8,128)(2,1)} %all-gather.3.cloned.1.call-done) | data formatting | bytes 12582912 | tf_op jit(solution)/shard_map/all_gather | solution.py:77
  284.8 5.8 %fusion = (f32[16,128]{1,0:T(8,128)S(1)}, f32[16,128,2048]{2,1,0:T(8,128)S(1)}) fusion(pred[128,2048]{1,0:T(8,128)(4,1)} %compare_and_fusion, bf16[128,16,96]{0,2,1:T(8,128)(2,1)S(1)} %bitcast.301, bf16[2048,16,96]{0,2,1:T(8,128)(2,1)} %bitcast.302), kind=kOutput, calls=%fused_computation.2 | convolution fusion | flops 817887232 | bytes 23732224 | tf_op jit(solution)/shard_map/shd,khd->hsk/dot_general | solution.py:47
  291.9 4.4 copy-done
  296.3 5.6 %fusion.1 = f32[16,128]{1,0:T(8,128)} fusion(f32[16,128,2048]{2,1,0:T(8,128)S(1)} %get-tuple-element.97, f32[16,128]{1,0:T(8,128)S(1)} %get-tuple-element.62, pred[128,2048]{1,0:T(8,128)(4,1)S(1)} %copy-done.6), kind=kLoop, calls=%fused_computation.3 | loop fusion | flops 20969472 | bytes 17055744 | tf_op jit(solution)/shard_map/reduce_sum | solution.py:53
  301.9 188.9 %all-gather.5.cloned.1.call-done = bf16[2048,1536]{1,0:T(8,128)(2,1)} async-done(((bf16[16,1536]{1,0:T(8,128)(2,1)}), bf16[2048,1536]{1,0:T(8,128)(2,1)}) %all-gather.5.cloned.1.call-update) | async-done | bytes 6291472 | tf_op jit(solution)/shard_map/all_gather | solution.py:78
  490.9 8.7 %copy.94 = bf16[2048,1536]{0,1:T(8,128)(2,1)} copy(bf16[2048,1536]{1,0:T(8,128)(2,1)} %all-gather.5.cloned.1.call-done) | data formatting | bytes 12582912 | tf_op jit(solution)/shard_map/all_gather | solution.py:78
  499.8 10.3 %fusion.38 = f32[128,16,96]{0,2,1:T(8,128)S(1)} fusion(bf16[2048,16,96]{0,2,1:T(8,128)(2,1)} %bitcast.305, f32[16,128,2048]{2,1,0:T(8,128)} %copy-done, f32[16,128]{1,0:T(8,128)} %copy-done.55, pred[128,2048]{1,0:T(8,128)(4,1)S(1)} %copy-done.7), kind=kOutput, calls=%fused_computation.59 | convolution fusion | flops 826277888 | bytes 24125440 | tf_op jit(solution)/shard_map/hsk,khd->hsd/dot_general | solution.py:54
  512.3 1.0 fusion.115
  513.3 0.9 bitcast_add_fusion
  514.2 1.1 fusion.37
  518.6 2.3 fusion.6
  520.9 23.1 %reduce-scatter.2.cloned.1.call-done = bf16[1536,128]{0,1:T(8,128)(2,1)} async-done(((bf16[3072,128]{0,1:T(8,128)(2,1)}), bf16[1536,128]{0,1:T(8,128)(2,1)}) %reduce-scatter.2.cloned.1.call-update) | async-done | bytes 393232 | tf_op jit(solution)/shard_map/reduce_scatter | solution.py:96
  544.0 1.9 copy.122
  (192 shorter events, 11.3 us)
Async XLA Ops:
  6.5 269.5 %all-gather.3.cloned.1.call-start = ((), (), s32[]{:S(2)}) async-start(), calls=%async_computation.1 | async-start | bytes 6340608 | tf_op jit(solution)/shard_map/all_gather | solution.py:77
  7.3 483.6 %all-gather.5.cloned.1.call-start = ((), (), s32[]{:S(2)}) async-start(), calls=%async_computation.2 | async-start | bytes 6340608 | tf_op jit(solution)/shard_map/all_gather | solution.py:78
  8.0 536.0 %reduce-scatter.2.cloned.1.call-start = ((), (), s32[]{:S(2)}) async-start(), calls=%async_computation.3 | async-start | bytes 1179648 | tf_op jit(solution)/shard_map/reduce_scatter | solution.py:96
  8.1 10.7 %collective-permute-start = (bf16[128,1536]{1,0:T(8,128)(2,1)}, bf16[128,1536]{1,0:T(8,128)(2,1)S(1)}, u32[]{:S(2)}, u32[]{:S(2)}) collective-permute-start(bf16[128,1536]{1,0:T(8,128)(2,1)} %param.11), channel_id=1, source_target_pairs={{0,2},{2,4},{4,6},{6,8},{8,10},{10,12},{12,14},{14,16},{16,18},{18... | collective-permute-start | bytes 1179656 | tf_op jit(solution)/shard_map/ppermute | solution.py:15
  13.0 9.7 %collective-permute-start.1 = (bf16[128,1536]{1,0:T(8,128)(2,1)}, bf16[128,1536]{1,0:T(8,128)(2,1)S(1)}, u32[]{:S(2)}, u32[]{:S(2)}) collective-permute-start(bf16[128,1536]{1,0:T(8,128)(2,1)} %param.12), channel_id=1, source_target_pairs={{0,2},{2,4},{4,6},{6,8},{8,10},{10,12},{12,14},{14,16},{16,18},{18... | collective-permute-start | bytes 1179656 | tf_op jit(solution)/shard_map/ppermute | solution.py:15
  17.5 42.1 %copy-start.57 = (pred[128,8]{0,1:T(8,128)(4,1)}, pred[128,8]{0,1:T(8,128)(4,1)S(1)}, u32[]{:S(2)}) copy-start(pred[128,8]{0,1:T(8,128)(4,1)S(1)} %broadcast_compare_fusion) | copy-start | bytes 3076
  18.7 40.9 %copy-start.27 = (pred[128,128]{0,1:T(8,128)(4,1)}, pred[128,128]{0,1:T(8,128)(4,1)S(1)}, u32[]{:S(2)}) copy-start(pred[128,128]{0,1:T(8,128)(4,1)S(1)} %get-tuple-element.69) | copy-start | bytes 49156
  18.7 11.3 %collective-permute-start.2 = (bf16[128,1536]{1,0:T(8,128)(2,1)S(1)}, bf16[128,1536]{1,0:T(8,128)(2,1)}, u32[]{:S(2)}, u32[]{:S(2)}) collective-permute-start(bf16[128,1536]{1,0:T(8,128)(2,1)S(1)} %collective-permute-done), channel_id=1, source_target_pairs={{0,2},{2,4},{4,6},{6,8},{8,10},{10,12},{12,14},{14,16},{16,18},{18... | collective-permute-start | bytes 1179656 | tf_op jit(solution)/shard_map/ppermute | solution.py:15
  22.7 10.5 %collective-permute-start.3 = (bf16[128,1536]{1,0:T(8,128)(2,1)S(1)}, bf16[128,1536]{1,0:T(8,128)(2,1)S(1)}, u32[]{:S(2)}, u32[]{:S(2)}) collective-permute-start(bf16[128,1536]{1,0:T(8,128)(2,1)S(1)} %collective-permute-done.1), channel_id=1, source_target_pairs={{0,2},{2,4},{4,6},{6,8},{8,10},{10,12},{12,14},{14,16},{16,18},{18... | collective-permute-start | bytes 1179656 | tf_op jit(solution)/shard_map/ppermute | solution.py:15
  30.0 13.1 %collective-permute-start.4 = (bf16[128,1536]{1,0:T(8,128)(2,1)}, bf16[128,1536]{1,0:T(8,128)(2,1)}, u32[]{:S(2)}, u32[]{:S(2)}) collective-permute-start(bf16[128,1536]{1,0:T(8,128)(2,1)} %collective-permute-done.2), channel_id=1, source_target_pairs={{0,2},{2,4},{4,6},{6,8},{8,10},{10,12},{12,14},{14,16},{16,18},{18... | collective-permute-start | bytes 1179656 | tf_op jit(solution)/shard_map/ppermute | solution.py:15
  33.2 26.5 %copy-start.19 = (bf16[128,1536]{1,0:T(8,128)(2,1)}, bf16[128,1536]{1,0:T(8,128)(2,1)S(1)}, u32[]{:S(2)}) copy-start(bf16[128,1536]{1,0:T(8,128)(2,1)S(1)} %collective-permute-done.3) | copy-start | bytes 1179652
  33.2 11.9 %collective-permute-start.5 = (bf16[128,1536]{1,0:T(8,128)(2,1)S(1)}, bf16[128,1536]{1,0:T(8,128)(2,1)}, u32[]{:S(2)}, u32[]{:S(2)}) collective-permute-start(bf16[128,1536]{1,0:T(8,128)(2,1)S(1)} %collective-permute-done.3), channel_id=1, source_target_pairs={{0,2},{2,4},{4,6},{6,8},{8,10},{10,12},{12,14},{14,16},{16,18},{18... | collective-permute-start | bytes 1179656 | tf_op jit(solution)/shard_map/ppermute | solution.py:15
  43.1 7.8 %collective-permute-start.6 = (bf16[128,1536]{1,0:T(8,128)(2,1)}, bf16[128,1536]{1,0:T(8,128)(2,1)}, u32[]{:S(2)}, u32[]{:S(2)}) collective-permute-start(bf16[128,1536]{1,0:T(8,128)(2,1)} %collective-permute-done.4), channel_id=1, source_target_pairs={{0,2},{2,4},{4,6},{6,8},{8,10},{10,12},{12,14},{14,16},{16,18},{18... | collective-permute-start | bytes 1179656 | tf_op jit(solution)/shard_map/ppermute | solution.py:15
  45.1 10.2 %collective-permute-start.7 = (bf16[128,1536]{1,0:T(8,128)(2,1)}, bf16[128,1536]{1,0:T(8,128)(2,1)}, u32[]{:S(2)}, u32[]{:S(2)}) collective-permute-start(bf16[128,1536]{1,0:T(8,128)(2,1)} %collective-permute-done.5), channel_id=1, source_target_pairs={{0,2},{2,4},{4,6},{6,8},{8,10},{10,12},{12,14},{14,16},{16,18},{18... | collective-permute-start | bytes 1179656 | tf_op jit(solution)/shard_map/ppermute | solution.py:15
  50.9 13.6 %collective-permute-start.8 = (bf16[128,1536]{1,0:T(8,128)(2,1)}, bf16[128,1536]{1,0:T(8,128)(2,1)}, u32[]{:S(2)}, u32[]{:S(2)}) collective-permute-start(bf16[128,1536]{1,0:T(8,128)(2,1)} %collective-permute-done.6), channel_id=1, source_target_pairs={{0,2},{2,4},{4,6},{6,8},{8,10},{10,12},{12,14},{14,16},{16,18},{18... | collective-permute-start | bytes 1179656 | tf_op jit(solution)/shard_map/ppermute | solution.py:15
  55.3 11.6 %collective-permute-start.9 = (bf16[128,1536]{1,0:T(8,128)(2,1)}, bf16[128,1536]{1,0:T(8,128)(2,1)}, u32[]{:S(2)}, u32[]{:S(2)}) collective-permute-start(bf16[128,1536]{1,0:T(8,128)(2,1)} %collective-permute-done.7), channel_id=1, source_target_pairs={{0,2},{2,4},{4,6},{6,8},{8,10},{10,12},{12,14},{14,16},{16,18},{18... | collective-permute-start | bytes 1179656 | tf_op jit(solution)/shard_map/ppermute | solution.py:15
  60.5 10.8 %copy-start.20 = (pred[128,128]{0,1:T(8,128)(4,1)}, pred[128,128]{0,1:T(8,128)(4,1)S(1)}, u32[]{:S(2)}) copy-start(pred[128,128]{0,1:T(8,128)(4,1)S(1)} %get-tuple-element.75) | copy-start | bytes 49156
  64.5 19.4 %collective-permute-start.10 = (bf16[128,1536]{1,0:T(8,128)(2,1)}, bf16[128,1536]{1,0:T(8,128)(2,1)}, u32[]{:S(2)}, u32[]{:S(2)}) collective-permute-start(bf16[128,1536]{1,0:T(8,128)(2,1)} %collective-permute-done.8), channel_id=1, source_target_pairs={{0,2},{2,4},{4,6},{6,8},{8,10},{10,12},{12,14},{14,16},{16,18},{18... | collective-permute-start | bytes 1179656 | tf_op jit(solution)/shard_map/ppermute | solution.py:15
  66.9 19.9 %collective-permute-start.11 = (bf16[128,1536]{1,0:T(8,128)(2,1)}, bf16[128,1536]{1,0:T(8,128)(2,1)}, u32[]{:S(2)}, u32[]{:S(2)}) collective-permute-start(bf16[128,1536]{1,0:T(8,128)(2,1)} %collective-permute-done.9), channel_id=1, source_target_pairs={{0,2},{2,4},{4,6},{6,8},{8,10},{10,12},{12,14},{14,16},{16,18},{18... | collective-permute-start | bytes 1179656 | tf_op jit(solution)/shard_map/ppermute | solution.py:15
  83.9 20.8 %collective-permute-start.12 = (bf16[128,1536]{1,0:T(8,128)(2,1)}, bf16[128,1536]{1,0:T(8,128)(2,1)}, u32[]{:S(2)}, u32[]{:S(2)}) collective-permute-start(bf16[128,1536]{1,0:T(8,128)(2,1)} %collective-permute-done.10), channel_id=1, source_target_pairs={{0,2},{2,4},{4,6},{6,8},{8,10},{10,12},{12,14},{14,16},{16,18},{18... | collective-permute-start | bytes 1179656 | tf_op jit(solution)/shard_map/ppermute | solution.py:15
  86.8 21.2 %collective-permute-start.13 = (bf16[128,1536]{1,0:T(8,128)(2,1)}, bf16[128,1536]{1,0:T(8,128)(2,1)}, u32[]{:S(2)}, u32[]{:S(2)}) collective-permute-start(bf16[128,1536]{1,0:T(8,128)(2,1)} %collective-permute-done.11), channel_id=1, source_target_pairs={{0,2},{2,4},{4,6},{6,8},{8,10},{10,12},{12,14},{14,16},{16,18},{18... | collective-permute-start | bytes 1179656 | tf_op jit(solution)/shard_map/ppermute | solution.py:15
  104.7 19.7 %collective-permute-start.14 = (bf16[128,1536]{1,0:T(8,128)(2,1)}, bf16[128,1536]{1,0:T(8,128)(2,1)}, u32[]{:S(2)}, u32[]{:S(2)}) collective-permute-start(bf16[128,1536]{1,0:T(8,128)(2,1)} %collective-permute-done.12), channel_id=1, source_target_pairs={{0,2},{2,4},{4,6},{6,8},{8,10},{10,12},{12,14},{14,16},{16,18},{18... | collective-permute-start | bytes 1179656 | tf_op jit(solution)/shard_map/ppermute | solution.py:15
  108.0 18.3 %collective-permute-start.15 = (bf16[128,1536]{1,0:T(8,128)(2,1)}, bf16[128,1536]{1,0:T(8,128)(2,1)}, u32[]{:S(2)}, u32[]{:S(2)}) collective-permute-start(bf16[128,1536]{1,0:T(8,128)(2,1)} %collective-permute-done.13), channel_id=1, source_target_pairs={{0,2},{2,4},{4,6},{6,8},{8,10},{10,12},{12,14},{14,16},{16,18},{18... | collective-permute-start | bytes 1179656 | tf_op jit(solution)/shard_map/ppermute | solution.py:15
  284.7 6.5 %copy-start.48 = (f32[16,128]{1,0:T(8,128)S(1)}, f32[16,128]{1,0:T(8,128)}, u32[]{:S(2)}) copy-start(f32[16,128]{1,0:T(8,128)} %get-tuple-element.84) | copy-start | bytes 24580
  284.7 6.5 %copy-start.51 = (f32[16,128]{1,0:T(8,128)S(1)}, f32[16,128]{1,0:T(8,128)}, u32[]{:S(2)}) copy-start(f32[16,128]{1,0:T(8,128)} %get-tuple-element.82) | copy-start | bytes 24580
  284.8 11.6 %copy-start.6 = (pred[128,2048]{1,0:T(8,128)(4,1)S(1)}, pred[128,2048]{1,0:T(8,128)(4,1)}, u32[]{:S(2)}) copy-start(pred[128,2048]{1,0:T(8,128)(4,1)} %compare_and_fusion) | copy-start | bytes 786436
  290.6 208.9 %copy-start.7 = (pred[128,2048]{1,0:T(8,128)(4,1)S(1)}, pred[128,2048]{1,0:T(8,128)(4,1)}, u32[]{:S(2)}) copy-start(pred[128,2048]{1,0:T(8,128)(4,1)} %compare_and_fusion) | copy-start | bytes 786436
  291.9 207.6 %copy-start.55 = (f32[16,128]{1,0:T(8,128)}, f32[16,128]{1,0:T(8,128)S(1)}, u32[]{:S(2)}) copy-start(f32[16,128]{1,0:T(8,128)S(1)} %get-tuple-element.62) | copy-start | bytes 24580
  499.5 10.6 %copy-start.8 = (f32[16,128,128]{1,2,0:T(8,128)S(1)}, f32[16,128,128]{1,2,0:T(8,128)}, u32[]{:S(2)}) copy-start(f32[16,128,128]{1,2,0:T(8,128)} %get-tuple-element.79) | copy-start | bytes 3145732
  499.5 10.6 %copy-start.29 = (pred[128,128]{0,1:T(8,128)(4,1)S(1)}, pred[128,128]{0,1:T(8,128)(4,1)}, u32[]{:S(2)}) copy-start(pred[128,128]{0,1:T(8,128)(4,1)} %get-tuple-element.76) | copy-start | bytes 49156
  499.5 10.6 %copy-start.56 = (f32[16,128]{1,0:T(8,128)S(1)}, f32[16,128]{1,0:T(8,128)}, u32[]{:S(2)}) copy-start(f32[16,128]{1,0:T(8,128)} %get-tuple-element.53) | copy-start | bytes 24580
  499.6 10.8 %copy-start.5 = (f32[16,128,128]{1,2,0:T(8,128)S(1)}, f32[16,128,128]{1,2,0:T(8,128)}, u32[]{:S(2)}) copy-start(f32[16,128,128]{1,2,0:T(8,128)} %get-tuple-element.81) | copy-start | bytes 3145732
  499.6 10.8 %copy-start.22 = (pred[128,128]{0,1:T(8,128)(4,1)S(1)}, pred[128,128]{0,1:T(8,128)(4,1)}, u32[]{:S(2)}) copy-start(pred[128,128]{0,1:T(8,128)(4,1)} %get-tuple-element.72) | copy-start | bytes 49156
  499.6 10.8 %copy-start.39 = (f32[16,128]{1,0:T(8,128)S(1)}, f32[16,128]{1,0:T(8,128)}, u32[]{:S(2)}) copy-start(f32[16,128]{1,0:T(8,128)} %get-tuple-element.54) | copy-start | bytes 24580
  499.6 11.0 %copy-start.4 = (f32[16,128,128]{1,2,0:T(8,128)S(1)}, f32[16,128,128]{1,2,0:T(8,128)}, u32[]{:S(2)}) copy-start(f32[16,128,128]{1,2,0:T(8,128)} %get-tuple-element.83) | copy-start | bytes 3145732
  499.6 11.0 %copy-start.23 = (pred[128,128]{0,1:T(8,128)(4,1)S(1)}, pred[128,128]{0,1:T(8,128)(4,1)}, u32[]{:S(2)}) copy-start(pred[128,128]{0,1:T(8,128)(4,1)} %get-tuple-element.74) | copy-start | bytes 49156
  499.6 11.0 %copy-start.40 = (f32[16,128]{1,0:T(8,128)S(1)}, f32[16,128]{1,0:T(8,128)}, u32[]{:S(2)}) copy-start(f32[16,128]{1,0:T(8,128)} %get-tuple-element.55) | copy-start | bytes 24580
  499.6 11.3 %copy-start.3 = (f32[16,128,128]{1,2,0:T(8,128)S(1)}, f32[16,128,128]{1,2,0:T(8,128)}, u32[]{:S(2)}) copy-start(f32[16,128,128]{1,2,0:T(8,128)} %get-tuple-element.85) | copy-start | bytes 3145732
  499.6 11.3 %copy-start.24 = (pred[128,128]{0,1:T(8,128)(4,1)S(1)}, pred[128,128]{0,1:T(8,128)(4,1)}, u32[]{:S(2)}) copy-start(pred[128,128]{0,1:T(8,128)(4,1)} %get-tuple-element.70) | copy-start | bytes 49156
  499.6 11.3 %copy-start.41 = (f32[16,128]{1,0:T(8,128)S(1)}, f32[16,128]{1,0:T(8,128)}, u32[]{:S(2)}) copy-start(f32[16,128]{1,0:T(8,128)} %get-tuple-element.56) | copy-start | bytes 24580
  499.6 11.5 %copy-start.2 = (f32[16,128,128]{1,2,0:T(8,128)S(1)}, f32[16,128,128]{1,2,0:T(8,128)}, u32[]{:S(2)}) copy-start(f32[16,128,128]{1,2,0:T(8,128)} %get-tuple-element.87) | copy-start | bytes 3145732
  499.7 11.5 %copy-start.42 = (f32[16,128]{1,0:T(8,128)S(1)}, f32[16,128]{1,0:T(8,128)}, u32[]{:S(2)}) copy-start(f32[16,128]{1,0:T(8,128)} %get-tuple-element.57) | copy-start | bytes 24580
  499.7 11.7 %copy-start.1 = (f32[16,128,128]{1,2,0:T(8,128)S(1)}, f32[16,128,128]{1,2,0:T(8,128)}, u32[]{:S(2)}) copy-start(f32[16,128,128]{1,2,0:T(8,128)} %get-tuple-element.89) | copy-start | bytes 3145732
  499.7 11.7 %copy-start.25 = (pred[128,128]{0,1:T(8,128)(4,1)S(1)}, pred[128,128]{0,1:T(8,128)(4,1)}, u32[]{:S(2)}) copy-start(pred[128,128]{0,1:T(8,128)(4,1)} %get-tuple-element.73) | copy-start | bytes 49156
  499.7 11.7 %copy-start.43 = (f32[16,128]{1,0:T(8,128)S(1)}, f32[16,128]{1,0:T(8,128)}, u32[]{:S(2)}) copy-start(f32[16,128]{1,0:T(8,128)} %get-tuple-element.58) | copy-start | bytes 24580
  499.7 11.9 %copy-start.26 = (pred[128,128]{0,1:T(8,128)(4,1)S(1)}, pred[128,128]{0,1:T(8,128)(4,1)}, u32[]{:S(2)}) copy-start(pred[128,128]{0,1:T(8,128)(4,1)} %get-tuple-element.71) | copy-start | bytes 49156
  499.7 11.9 %copy-start.44 = (f32[16,128]{1,0:T(8,128)S(1)}, f32[16,128]{1,0:T(8,128)}, u32[]{:S(2)}) copy-start(f32[16,128]{1,0:T(8,128)} %get-tuple-element.59) | copy-start | bytes 24580
  499.7 12.1 %copy-start.21 = (pred[128,128]{0,1:T(8,128)(4,1)S(1)}, pred[128,128]{0,1:T(8,128)(4,1)}, u32[]{:S(2)}) copy-start(pred[128,128]{0,1:T(8,128)(4,1)} %copy-done.20) | copy-start | bytes 49156
  499.7 12.1 %copy-start.45 = (f32[16,128]{1,0:T(8,128)S(1)}, f32[16,128]{1,0:T(8,128)}, u32[]{:S(2)}) copy-start(f32[16,128]{1,0:T(8,128)} %get-tuple-element.60) | copy-start | bytes 24580
  499.7 12.3 %copy-start.28 = (pred[128,128]{0,1:T(8,128)(4,1)S(1)}, pred[128,128]{0,1:T(8,128)(4,1)}, u32[]{:S(2)}) copy-start(pred[128,128]{0,1:T(8,128)(4,1)} %copy-done.27) | copy-start | bytes 49156
  499.7 12.3 %copy-start.46 = (f32[16,128]{1,0:T(8,128)S(1)}, f32[16,128]{1,0:T(8,128)}, u32[]{:S(2)}) copy-start(f32[16,128]{1,0:T(8,128)} %get-tuple-element.61) | copy-start | bytes 24580
  499.8 12.5 %copy-start.17 = (f32[16,128,8]{1,2,0:T(8,128)S(1)}, f32[16,128,8]{1,2,0:T(8,128)}, u32[]{:S(2)}) copy-start(f32[16,128,8]{1,2,0:T(8,128)} %get-tuple-element.99) | copy-start | bytes 196612
  499.8 13.5 %copy-start.31 = (f32[16,128]{1,0:T(8,128)S(1)}, f32[16,128]{1,0:T(8,128)}, u32[]{:S(2)}) copy-start(f32[16,128]{1,0:T(8,128)} %get-tuple-element.98) | copy-start | bytes 24580
  499.8 13.5 %copy-start.33 = (f32[16,128]{1,0:T(8,128)S(1)}, f32[16,128]{1,0:T(8,128)}, u32[]{:S(2)}) copy-start(f32[16,128]{1,0:T(8,128)} %get-tuple-element.92) | copy-start | bytes 24580
  499.8 13.5 %copy-start.35 = (f32[16,128]{1,0:T(8,128)S(1)}, f32[16,128]{1,0:T(8,128)}, u32[]{:S(2)}) copy-start(f32[16,128]{1,0:T(8,128)} %get-tuple-element.88) | copy-start | bytes 24580
  499.8 13.5 %copy-start.37 = (f32[16,128]{1,0:T(8,128)S(1)}, f32[16,128]{1,0:T(8,128)}, u32[]{:S(2)}) copy-start(f32[16,128]{1,0:T(8,128)} %copy-done.36) | copy-start | bytes 24580
  499.8 13.5 %copy-start.49 = (f32[16,128]{1,0:T(8,128)S(1)}, f32[16,128]{1,0:T(8,128)}, u32[]{:S(2)}) copy-start(f32[16,128]{1,0:T(8,128)} %get-tuple-element.84) | copy-start | bytes 24580
  499.8 14.3 %copy-start.38 = (bf16[8,16,96]{2,1,0:T(8,128)(2,1)S(1)}, bf16[8,16,96]{2,1,0:T(8,128)(2,1)}, u32[]{:S(2)}) copy-start(bf16[8,16,96]{2,1,0:T(8,128)(2,1)} %reshape.1640) | copy-start | bytes 73732
  499.8 15.4 %copy-start.9 = (bf16[128,1536]{0,1:T(8,128)(2,1)S(1)}, bf16[128,1536]{0,1:T(8,128)(2,1)}, u32[]{:S(2)}) copy-start(bf16[128,1536]{0,1:T(8,128)(2,1)} %copy.96) | copy-start | bytes 1179652
  499.8 15.7 %copy-start.10 = (bf16[128,1536]{0,1:T(8,128)(2,1)S(1)}, bf16[128,1536]{0,1:T(8,128)(2,1)}, u32[]{:S(2)}) copy-start(bf16[128,1536]{0,1:T(8,128)(2,1)} %copy.99) | copy-start | bytes 1179652
  510.1 6.7 %copy-start.13 = (bf16[128,1536]{0,1:T(8,128)(2,1)S(1)}, bf16[128,1536]{0,1:T(8,128)(2,1)}, u32[]{:S(2)}) copy-start(bf16[128,1536]{0,1:T(8,128)(2,1)} %copy.111) | copy-start | bytes 1179652
  510.1 7.0 %copy-start.16 = (bf16[128,1536]{0,1:T(8,128)(2,1)S(1)}, bf16[128,1536]{0,1:T(8,128)(2,1)}, u32[]{:S(2)}) copy-start(bf16[128,1536]{0,1:T(8,128)(2,1)} %copy.114) | copy-start | bytes 1179652
  510.2 7.4 %copy-start.15 = (bf16[128,1536]{0,1:T(8,128)(2,1)S(1)}, bf16[128,1536]{0,1:T(8,128)(2,1)}, u32[]{:S(2)}) copy-start(bf16[128,1536]{0,1:T(8,128)(2,1)} %copy.117) | copy-start | bytes 1179652
  510.7 7.2 %copy-start.18 = (bf16[128,1536]{0,1:T(8,128)(2,1)S(1)}, bf16[128,1536]{0,1:T(8,128)(2,1)}, u32[]{:S(2)}) copy-start(bf16[128,1536]{0,1:T(8,128)(2,1)} %copy.120) | copy-start | bytes 1179652
  (16 other events, 84.4 us)
Sparse Core Ops, SparseCore 0:
  9.2 266.7 all-gather.2
  277.9 212.9 all-gather.4
  521.1 22.9 reduce-scatter.1
where the time goes:
time: 554 us; the launch traced here: 552 us
  waiting for transfers between devices  360 us (65%)
  local copies, waits for them, and re-layouts  59.7 us (11%)
  starting transfers between devices  58.2 us (11%)
  matrix products  45.1 us (8%)
  other arithmetic  15.2 us (3%)
  between operations  14.5 us (3%)
    all_gather x1, waiting for transfers between devices, shards(): lax.all_gather(cache_v, 'seq', axis=0, tiled=True)  189 us
    all_gather x1, waiting for transfers between devices, shards(): lax.all_gather(cache_k, 'seq', axis=0, tiled=True)  145 us
    ppermute x16, starting transfers between devices, from_behind(): return lax.ppermute(array, axis, pairs)  58.1 us
    dot_general x11, matrix products, absorb(): jnp.einsum('shd,khd->hsk', q_three, k_three, preferred_element_type=jnp.f...  28.8 us
    ppermute x16, local copies, waits for them, and re-layouts, from_behind(): return lax.ppermute(array, axis, pairs)  28 us
    reduce_scatter x1, waiting for transfers between devices, shards(): lax.psum_scatter(jnp.einsum('cd,sc->ds', w_out, attn, preferred_element_t...  23.1 us
    dot_general x11, matrix products, absorb(): jnp.einsum('hsk,khd->hsd', prob.astype(jnp.bfloat16), v_three, preferred_...  14.1 us
  transfers between devices with their start and end apart: 19, of which 5 were waited for; matrix products, arithmetic and copies ran while one was open for 15% of the time, Pallas kernels for 0%

commit v1 on v0

--- a/solution.py
+++ b/solution.py
@@ -73,10 +73,16 @@
     )
     sink_group = jnp.arange(sink_k.shape[0], dtype=jnp.int32) // SINKS
     state = absorb(state, sink_k, sink_v, grp_q[:, None] == sink_group[None, :])
-    pieces = (
-        lax.all_gather(cache_k, "seq", axis=0, tiled=True),
-        lax.all_gather(cache_v, "seq", axis=0, tiled=True),
-    )
+
+    def space_perform(v0):
+        return jnp.concatenate(
+            lax.all_to_all(
+                jnp.stack([v0] * lax.axis_size("seq")), axis_name="seq", split_axis=0, concat_axis=0
+            ),
+            0,
+        )
+
+    pieces = (space_perform(cache_k), lax.all_gather(cache_v, "seq", axis=0, tiled=True))
     slot = jnp.arange(pieces[0].shape[0], dtype=jnp.int32)
     state = absorb(
         state,

time: 554 us -> 381 us (0.69)
  waiting for transfers between devices: 360 us -> 176 us
  starting transfers between devices: 58.2 us -> 74.7 us
  local copies, waits for them, and re-layouts: 59.7 us -> 53.8 us
    all_gather x1, waiting for transfers between devices: 189 us -> 0.01 us  [shards(): lax.all_gather(cache_v, 'seq', axis=0, tiled=True)]
    ppermute x16, waiting for transfers between devices: 1.49 us -> 153 us  [from_behind(): return lax.ppermute(array, axis, pairs)]
    all_gather x1 -> x0, waiting for transfers between devices: 145 us -> none  [shards(): lax.all_gather(cache_k, 'seq', axis=0, tiled=True)]
    another operation x1 -> x3, local copies, waits for them, and re-layouts: 0.74 us -> 18.1 us  [the longest x1 13.6 us: absorb(): k_three = key_rows.reshape(count, heads, HD)]
    all_to_all x0 -> x1, starting transfers between devices: none -> 15.3 us  [space_perform(): lax.all_to_all(jnp.stack([v0] * lax.axis_size('seq')), axis_name='seq', s...]
    all_gather x1 -> x0, local copies, waits for them, and re-layouts: 8.66 us -> none  [shards(): lax.all_gather(cache_k, 'seq', axis=0, tiled=True)]
    ppermute x16, local copies, waits for them, and re-layouts: 28 us -> 21.1 us  [from_behind(): return lax.ppermute(array, axis, pairs)]
    unnamed x125 -> x115, local copies, waits for them, and re-layouts: 9.45 us -> 3.23 us
  transfers between devices with their start and end apart: 19 -> 19, of which waited for: 5 -> 6; matrix products, arithmetic and copies ran while one was open for 15% -> 20% of each run, Pallas kernels for 0% -> 0%
where the time goes in v1:
time: 381 us; the launch traced here: 379 us
  waiting for transfers between devices  176 us (46%)
  starting transfers between devices  74.7 us (20%)
  local copies, waits for them, and re-layouts  53.8 us (14%)
  matrix products  42.2 us (11%)
  other arithmetic  17 us (4%)
  between operations  14.8 us (4%)
    ppermute x16, waiting for transfers between devices, from_behind(): return lax.ppermute(array, axis, pairs)  153 us
    ppermute x16, starting transfers between devices, from_behind(): return lax.ppermute(array, axis, pairs)  59.4 us
    dot_general x11, matrix products, absorb(): jnp.einsum('shd,khd->hsk', q_three, k_three, preferred_element_type=jnp.f...  25.9 us
    reduce_scatter x1, waiting for transfers between devices, shards(): lax.psum_scatter(jnp.einsum('cd,sc->ds', w_out, attn, preferred_element_t...  22.3 us
    ppermute x16, local copies, waits for them, and re-layouts, from_behind(): return lax.ppermute(array, axis, pairs)  21.1 us
    all_to_all x1, starting transfers between devices, space_perform(): lax.all_to_all(jnp.stack([v0] * lax.axis_size('seq')), axis_name='seq', s...  15.3 us
    dot_general x11, matrix products, absorb(): jnp.einsum('hsk,khd->hsd', prob.astype(jnp.bfloat16), v_three, preferred_...  14 us
    another operation x1, local copies, waits for them, and re-layouts, absorb(): k_three = key_rows.reshape(count, heads, HD)  13.6 us
  transfers between devices with their start and end apart: 19, of which 6 were waited for; matrix products, arithmetic and copies ran while one was open for 20% of the time, Pallas kernels for 0%

profile of v1, /device:TPU:1, one launch (start us, length us, event | category | flops | bytes accessed | tf_op | source)
XLA Modules:
  0.0 378.7 jit_solution(4675555581239065956)
XLA Ops:
  6.6 4.3 %stack.2 = bf16[128,16,1536]{2,1,0:T(8,128)(2,1)} broadcast(bf16[16,1536]{1,0:T(8,128)(2,1)} %param.13), dimensions={1,2} | broadcast | bytes 6340608 | tf_op jit(solution)/shard_map/stack | solution.py:80
  10.9 15.3 %all-to-all-start = ((bf16[128,16,1536]{2,1,0:T(8,128)(2,1)}), bf16[128,16,1536]{2,1,0:T(8,128)(2,1)}, u32[]{:S(2)}, u32[]{:S(2)}) async-start(bf16[128,16,1536]{2,1,0:T(8,128)(2,1)} %stack.2), calls=%async_computation | async-start | bytes 12582912 | tf_op jit(solution)/shard_map/all_to_all | solution.py:79
  26.2 0.7 all-gather.2.cloned.1.call-update
  27.0 3.5 collective-permute-start
  30.5 2.0 collective-permute-start.1
  33.7 150.8 %collective-permute-done = bf16[128,1536]{1,0:T(8,128)(2,1)S(1)} collective-permute-done((bf16[128,1536]{1,0:T(8,128)(2,1)S(1)}, bf16[128,1536]{1,0:T(8,128)(2,1)S(1)}, u32[]{:S(2)}, u32[]{:S(2)}) %collective-permute-start) | collective-permute-done | bytes 393248 | tf_op jit(solution)/shard_map/ppermute | solution.py:15
  184.5 4.4 %collective-permute-start.2 = (bf16[128,1536]{1,0:T(8,128)(2,1)S(1)}, bf16[128,1536]{1,0:T(8,128)(2,1)}, u32[]{:S(2)}, u32[]{:S(2)}) collective-permute-start(bf16[128,1536]{1,0:T(8,128)(2,1)S(1)} %collective-permute-done), channel_id=1, source_target_pairs={{0,2},{2,4},{4,6},{6,8},{8,10},{10,12},{12,14},{14,16},{16,18},{18... | collective-permute-start | bytes 1179656 | tf_op jit(solution)/shard_map/ppermute | solution.py:15
  188.9 0.6 collective-permute-done.1
  189.4 4.4 %collective-permute-start.3 = (bf16[128,1536]{1,0:T(8,128)(2,1)S(1)}, bf16[128,1536]{1,0:T(8,128)(2,1)}, u32[]{:S(2)}, u32[]{:S(2)}) collective-permute-start(bf16[128,1536]{1,0:T(8,128)(2,1)S(1)} %collective-permute-done.1), channel_id=1, source_target_pairs={{0,2},{2,4},{4,6},{6,8},{8,10},{10,12},{12,14},{14,16},{16,18},{18... | collective-permute-start | bytes 1179656 | tf_op jit(solution)/shard_map/ppermute | solution.py:15
  194.4 3.8 collective-permute-start.4
  198.2 1.0 collective-permute-done.3
  199.1 4.6 %collective-permute-start.5 = (bf16[128,1536]{1,0:T(8,128)(2,1)}, bf16[128,1536]{1,0:T(8,128)(2,1)}, u32[]{:S(2)}, u32[]{:S(2)}) collective-permute-start(bf16[128,1536]{1,0:T(8,128)(2,1)} %collective-permute-done.3), channel_id=1, source_target_pairs={{0,2},{2,4},{4,6},{6,8},{8,10},{10,12},{12,14},{14,16},{16,18},{18... | collective-permute-start | bytes 1179656 | tf_op jit(solution)/shard_map/ppermute | solution.py:15
  204.0 0.9 copy.96
  204.9 0.7 reshape.1639
  205.6 1.0 fusion.172
  206.6 1.9 collective-permute-start.6
  208.5 0.8 collective-permute-done.5
  209.3 4.4 %collective-permute-start.7 = (bf16[128,1536]{1,0:T(8,128)(2,1)}, bf16[128,1536]{1,0:T(8,128)(2,1)S(1)}, u32[]{:S(2)}, u32[]{:S(2)}) collective-permute-start(bf16[128,1536]{1,0:T(8,128)(2,1)} %collective-permute-done.5), channel_id=1, source_target_pairs={{0,2},{2,4},{4,6},{6,8},{8,10},{10,12},{12,14},{14,16},{16,18},{18... | collective-permute-start | bytes 1179656 | tf_op jit(solution)/shard_map/ppermute | solution.py:15
  213.7 1.0 compare_and_fusion
  214.7 3.9 %collective-permute-start.8 = (bf16[128,1536]{1,0:T(8,128)(2,1)}, bf16[128,1536]{1,0:T(8,128)(2,1)}, u32[]{:S(2)}, u32[]{:S(2)}) collective-permute-start(bf16[128,1536]{1,0:T(8,128)(2,1)} %collective-permute-done.6), channel_id=1, source_target_pairs={{0,2},{2,4},{4,6},{6,8},{8,10},{10,12},{12,14},{14,16},{16,18},{18... | collective-permute-start | bytes 1179656 | tf_op jit(solution)/shard_map/ppermute | solution.py:15
  218.7 4.3 %collective-permute-start.9 = (bf16[128,1536]{1,0:T(8,128)(2,1)S(1)}, bf16[128,1536]{1,0:T(8,128)(2,1)}, u32[]{:S(2)}, u32[]{:S(2)}) collective-permute-start(bf16[128,1536]{1,0:T(8,128)(2,1)S(1)} %collective-permute-done.7), channel_id=1, source_target_pairs={{0,2},{2,4},{4,6},{6,8},{8,10},{10,12},{12,14},{14,16},{16,18},{18... | collective-permute-start | bytes 1179656 | tf_op jit(solution)/shard_map/ppermute | solution.py:15
  223.4 0.9 copy.99
  224.4 1.0 fusion.171
  225.4 1.2 copy.101
  226.6 2.1 collective-permute-start.10
  228.7 4.3 %collective-permute-start.11 = (bf16[128,1536]{1,0:T(8,128)(2,1)}, bf16[128,1536]{1,0:T(8,128)(2,1)}, u32[]{:S(2)}, u32[]{:S(2)}) collective-permute-start(bf16[128,1536]{1,0:T(8,128)(2,1)} %collective-permute-done.9), channel_id=1, source_target_pairs={{0,2},{2,4},{4,6},{6,8},{8,10},{10,12},{12,14},{14,16},{16,18},{18... | collective-permute-start | bytes 1179656 | tf_op jit(solution)/shard_map/ppermute | solution.py:15
  233.1 2.0 fusion.170
  235.1 1.9 copy.102
  237.0 1.2 copy.104
  238.2 1.9 copy.105
  240.1 1.9 fusion.169
  242.1 1.2 copy.107
  243.3 2.3 collective-permute-start.12
  245.6 4.3 %collective-permute-start.13 = (bf16[128,1536]{1,0:T(8,128)(2,1)}, bf16[128,1536]{1,0:T(8,128)(2,1)}, u32[]{:S(2)}, u32[]{:S(2)}) collective-permute-start(bf16[128,1536]{1,0:T(8,128)(2,1)} %collective-permute-done.11), channel_id=1, source_target_pairs={{0,2},{2,4},{4,6},{6,8},{8,10},{10,12},{12,14},{14,16},{16,18},{18... | collective-permute-start | bytes 1179656 | tf_op jit(solution)/shard_map/ppermute | solution.py:15
  249.9 1.9 fusion.168
  251.8 0.9 copy.108
  252.8 1.2 copy.110
  254.0 1.9 copy.111
  255.9 2.0 fusion.167
  257.9 1.2 copy.113
  259.1 4.7 %collective-permute-start.14 = (bf16[128,1536]{1,0:T(8,128)(2,1)}, bf16[128,1536]{1,0:T(8,128)(2,1)S(1)}, u32[]{:S(2)}, u32[]{:S(2)}) collective-permute-start(bf16[128,1536]{1,0:T(8,128)(2,1)} %collective-permute-done.12), channel_id=1, source_target_pairs={{0,2},{2,4},{4,6},{6,8},{8,10},{10,12},{12,14},{14,16},{16,18},{18... | collective-permute-start | bytes 1179656 | tf_op jit(solution)/shard_map/ppermute | solution.py:15
  263.8 4.6 %collective-permute-start.15 = (bf16[128,1536]{1,0:T(8,128)(2,1)}, bf16[128,1536]{1,0:T(8,128)(2,1)}, u32[]{:S(2)}, u32[]{:S(2)}) collective-permute-start(bf16[128,1536]{1,0:T(8,128)(2,1)} %collective-permute-done.13), channel_id=1, source_target_pairs={{0,2},{2,4},{4,6},{6,8},{8,10},{10,12},{12,14},{14,16},{16,18},{18... | collective-permute-start | bytes 1179656 | tf_op jit(solution)/shard_map/ppermute | solution.py:15
  268.4 1.9 fusion.166
  270.3 1.9 copy.114
  272.3 1.2 copy.116
  273.5 1.9 copy.117
  275.4 2.0 fusion.165
  277.6 1.9 copy.120
  279.5 1.9 fusion.164
  281.5 13.6 %reshape_reshape.3 = bf16[2048,16,96]{2,1,0:T(8,128)(2,1)} reshape(bf16[128,16,1536]{2,1,0:T(8,128)(2,1)} %all-to-all-done) | data formatting | bytes 12582912 | tf_op jit(solution)/shard_map/reshape;reshape | solution.py:44
  295.1 10.1 %fusion = (f32[16,128]{1,0:T(8,128)}, f32[16,128,2048]{2,1,0:T(8,128)S(1)}) fusion(pred[128,2048]{1,0:T(8,128)(4,1)} %compare_and_fusion, bf16[128,16,96]{0,2,1:T(8,128)(2,1)S(1)} %bitcast.299, bf16[2048,16,96]{2,1,0:T(8,128)(2,1)} %reshape_reshape.3), kind=kOutput, calls=%fused_computation.2 | convolution fusion | flops 817887232 | bytes 23732224 | tf_op jit(solution)/shard_map/shd,khd->hsk/dot_general | solution.py:47
  305.2 2.2 bitcast_maximum_fusion.3
  307.4 2.5 fusion.162
  310.0 1.2 copy-done
  311.2 6.6 %fusion.1 = f32[16,128]{1,0:T(8,128)} fusion(f32[16,128,2048]{2,1,0:T(8,128)S(1)} %get-tuple-element.97, f32[16,128]{1,0:T(8,128)S(1)} %get-tuple-element.62, pred[128,2048]{1,0:T(8,128)(4,1)} %compare_and_fusion), kind=kLoop, calls=%fused_computation.3 | loop fusion | flops 20969472 | bytes 17055744 | tf_op jit(solution)/shard_map/reduce_sum | solution.py:53
  317.8 8.7 %copy.94 = bf16[2048,1536]{0,1:T(8,128)(2,1)} copy(bf16[2048,1536]{1,0:T(8,128)(2,1)} %all-gather.2.cloned.1.call-done) | data formatting | bytes 12582912 | tf_op jit(solution)/shard_map/all_gather | solution.py:85
  326.8 10.3 %fusion.40 = f32[128,16,96]{0,2,1:T(8,128)S(1)} fusion(bf16[2048,16,96]{0,2,1:T(8,128)(2,1)} %bitcast.302, f32[16,128,2048]{2,1,0:T(8,128)} %copy-done, f32[16,128]{1,0:T(8,128)} %copy-done.46, pred[128,2048]{1,0:T(8,128)(4,1)S(1)} %copy-done.7), kind=kOutput, calls=%fused_computation.61 | convolution fusion | flops 826277888 | bytes 24125440 | tf_op jit(solution)/shard_map/hsk,khd->hsd/dot_general | solution.py:54
  339.1 0.9 fusion.117
  340.2 0.8 bitcast_add_fusion
  341.0 1.0 fusion.39
  345.0 0.4 slice-done.2
  345.4 2.3 fusion.8
  347.7 22.3 %reduce-scatter.2.cloned.1.call-done = bf16[1536,128]{0,1:T(8,128)(2,1)} async-done(((bf16[3072,128]{0,1:T(8,128)(2,1)}), bf16[1536,128]{0,1:T(8,128)(2,1)}) %reduce-scatter.2.cloned.1.call-update) | async-done | bytes 393232 | tf_op jit(solution)/shard_map/reduce_scatter | solution.py:102
  370.0 1.9 copy.122
  (182 shorter events, 7.4 us)
Async XLA Ops:
  6.5 20.4 %copy-start.18 = (bf16[128,1536]{1,0:T(8,128)(2,1)S(1)}, bf16[128,1536]{1,0:T(8,128)(2,1)}, u32[]{:S(2)}) copy-start(bf16[128,1536]{1,0:T(8,128)(2,1)} %param.11) | copy-start | bytes 1179652
  6.5 24.0 %copy-start.19 = (bf16[128,1536]{1,0:T(8,128)(2,1)S(1)}, bf16[128,1536]{1,0:T(8,128)(2,1)}, u32[]{:S(2)}) copy-start(bf16[128,1536]{1,0:T(8,128)(2,1)} %param.12) | copy-start | bytes 1179652
  6.5 26.0 %copy-start.51 = (s32[32]{0:T(128)S(1)}, s32[32]{0:T(128)}, u32[]{:S(2)}) copy-start(s32[32]{0:T(128)} %param.17) | copy-start | bytes 388
  6.5 26.4 %copy-start.52 = (s32[32]{0:T(128)S(1)}, s32[32]{0:T(128)}, u32[]{:S(2)}) copy-start(s32[32]{0:T(128)} %param.18) | copy-start | bytes 388
  6.5 187.3 %copy-start.17 = (bf16[128,1536]{1,0:T(8,128)(2,1)S(1)}, bf16[128,1536]{1,0:T(8,128)(2,1)}, u32[]{:S(2)}) copy-start(bf16[128,1536]{1,0:T(8,128)(2,1)} %param.10) | copy-start | bytes 1179652
  6.5 187.5 %copy-start.48 = (bf16[8,1536]{1,0:T(8,128)(2,1)S(1)}, bf16[8,1536]{1,0:T(8,128)(2,1)}, u32[]{:S(2)}) copy-start(bf16[8,1536]{1,0:T(8,128)(2,1)} %param.15) | copy-start | bytes 73732
  6.6 198.3 %copy-start.49 = (bf16[8,1536]{1,0:T(8,128)(2,1)S(1)}, bf16[8,1536]{1,0:T(8,128)(2,1)}, u32[]{:S(2)}) copy-start(bf16[8,1536]{1,0:T(8,128)(2,1)} %param.16) | copy-start | bytes 73732
  10.9 270.5 %all-to-all-start = ((bf16[128,16,1536]{2,1,0:T(8,128)(2,1)}), bf16[128,16,1536]{2,1,0:T(8,128)(2,1)}, u32[]{:S(2)}, u32[]{:S(2)}) async-start(bf16[128,16,1536]{2,1,0:T(8,128)(2,1)} %stack.2), calls=%async_computation | async-start | bytes 12582912 | tf_op jit(solution)/shard_map/all_to_all | solution.py:79
  26.2 291.6 %all-gather.2.cloned.1.call-start = ((), (), s32[]{:S(2)}) async-start(), calls=%async_computation.2 | async-start | bytes 6340608 | tf_op jit(solution)/shard_map/all_gather | solution.py:85
  26.9 343.1 %reduce-scatter.2.cloned.1.call-start = ((), (), s32[]{:S(2)}) async-start(), calls=%async_computation.3 | async-start | bytes 1179648 | tf_op jit(solution)/shard_map/reduce_scatter | solution.py:102
  27.0 157.5 %collective-permute-start = (bf16[128,1536]{1,0:T(8,128)(2,1)S(1)}, bf16[128,1536]{1,0:T(8,128)(2,1)S(1)}, u32[]{:S(2)}, u32[]{:S(2)}) collective-permute-start(bf16[128,1536]{1,0:T(8,128)(2,1)S(1)} %copy-done.18), channel_id=1, source_target_pairs={{0,2},{2,4},{4,6},{6,8},{8,10},{10,12},{12,14},{14,16},{16,18},{18... | collective-permute-start | bytes 1179656 | tf_op jit(solution)/shard_map/ppermute | solution.py:15
  30.5 158.9 %collective-permute-start.1 = (bf16[128,1536]{1,0:T(8,128)(2,1)S(1)}, bf16[128,1536]{1,0:T(8,128)(2,1)S(1)}, u32[]{:S(2)}, u32[]{:S(2)}) collective-permute-start(bf16[128,1536]{1,0:T(8,128)(2,1)S(1)} %copy-done.19), channel_id=1, source_target_pairs={{0,2},{2,4},{4,6},{6,8},{8,10},{10,12},{12,14},{14,16},{16,18},{18... | collective-permute-start | bytes 1179656 | tf_op jit(solution)/shard_map/ppermute | solution.py:15
  33.2 248.2 %copy-start.50 = (pred[128,8]{0,1:T(8,128)(4,1)}, pred[128,8]{0,1:T(8,128)(4,1)S(1)}, u32[]{:S(2)}) copy-start(pred[128,8]{0,1:T(8,128)(4,1)S(1)} %broadcast_compare_fusion) | copy-start | bytes 3076
  33.7 189.3 %copy-start.25 = (pred[128,128]{0,1:T(8,128)(4,1)}, pred[128,128]{0,1:T(8,128)(4,1)S(1)}, u32[]{:S(2)}) copy-start(pred[128,128]{0,1:T(8,128)(4,1)S(1)} %get-tuple-element.69) | copy-start | bytes 49156
  33.7 247.8 %copy-start.21 = (pred[128,128]{0,1:T(8,128)(4,1)}, pred[128,128]{0,1:T(8,128)(4,1)S(1)}, u32[]{:S(2)}) copy-start(pred[128,128]{0,1:T(8,128)(4,1)S(1)} %get-tuple-element.73) | copy-start | bytes 49156
  33.7 247.8 %copy-start.23 = (pred[128,128]{0,1:T(8,128)(4,1)}, pred[128,128]{0,1:T(8,128)(4,1)S(1)}, u32[]{:S(2)}) copy-start(pred[128,128]{0,1:T(8,128)(4,1)S(1)} %get-tuple-element.71) | copy-start | bytes 49156
  184.5 9.9 %collective-permute-start.2 = (bf16[128,1536]{1,0:T(8,128)(2,1)S(1)}, bf16[128,1536]{1,0:T(8,128)(2,1)}, u32[]{:S(2)}, u32[]{:S(2)}) collective-permute-start(bf16[128,1536]{1,0:T(8,128)(2,1)S(1)} %collective-permute-done), channel_id=1, source_target_pairs={{0,2},{2,4},{4,6},{6,8},{8,10},{10,12},{12,14},{14,16},{16,18},{18... | collective-permute-start | bytes 1179656 | tf_op jit(solution)/shard_map/ppermute | solution.py:15
  189.4 9.7 %collective-permute-start.3 = (bf16[128,1536]{1,0:T(8,128)(2,1)S(1)}, bf16[128,1536]{1,0:T(8,128)(2,1)}, u32[]{:S(2)}, u32[]{:S(2)}) collective-permute-start(bf16[128,1536]{1,0:T(8,128)(2,1)S(1)} %collective-permute-done.1), channel_id=1, source_target_pairs={{0,2},{2,4},{4,6},{6,8},{8,10},{10,12},{12,14},{14,16},{16,18},{18... | collective-permute-start | bytes 1179656 | tf_op jit(solution)/shard_map/ppermute | solution.py:15
  194.4 12.2 %collective-permute-start.4 = (bf16[128,1536]{1,0:T(8,128)(2,1)}, bf16[128,1536]{1,0:T(8,128)(2,1)}, u32[]{:S(2)}, u32[]{:S(2)}) collective-permute-start(bf16[128,1536]{1,0:T(8,128)(2,1)} %collective-permute-done.2), channel_id=1, source_target_pairs={{0,2},{2,4},{4,6},{6,8},{8,10},{10,12},{12,14},{14,16},{16,18},{18... | collective-permute-start | bytes 1179656 | tf_op jit(solution)/shard_map/ppermute | solution.py:15
  199.1 10.1 %collective-permute-start.5 = (bf16[128,1536]{1,0:T(8,128)(2,1)}, bf16[128,1536]{1,0:T(8,128)(2,1)}, u32[]{:S(2)}, u32[]{:S(2)}) collective-permute-start(bf16[128,1536]{1,0:T(8,128)(2,1)} %collective-permute-done.3), channel_id=1, source_target_pairs={{0,2},{2,4},{4,6},{6,8},{8,10},{10,12},{12,14},{14,16},{16,18},{18... | collective-permute-start | bytes 1179656 | tf_op jit(solution)/shard_map/ppermute | solution.py:15
  206.6 8.1 %collective-permute-start.6 = (bf16[128,1536]{1,0:T(8,128)(2,1)}, bf16[128,1536]{1,0:T(8,128)(2,1)}, u32[]{:S(2)}, u32[]{:S(2)}) collective-permute-start(bf16[128,1536]{1,0:T(8,128)(2,1)} %collective-permute-done.4), channel_id=1, source_target_pairs={{0,2},{2,4},{4,6},{6,8},{8,10},{10,12},{12,14},{14,16},{16,18},{18... | collective-permute-start | bytes 1179656 | tf_op jit(solution)/shard_map/ppermute | solution.py:15
  209.3 9.4 %collective-permute-start.7 = (bf16[128,1536]{1,0:T(8,128)(2,1)}, bf16[128,1536]{1,0:T(8,128)(2,1)S(1)}, u32[]{:S(2)}, u32[]{:S(2)}) collective-permute-start(bf16[128,1536]{1,0:T(8,128)(2,1)} %collective-permute-done.5), channel_id=1, source_target_pairs={{0,2},{2,4},{4,6},{6,8},{8,10},{10,12},{12,14},{14,16},{16,18},{18... | collective-permute-start | bytes 1179656 | tf_op jit(solution)/shard_map/ppermute | solution.py:15
  214.7 11.9 %collective-permute-start.8 = (bf16[128,1536]{1,0:T(8,128)(2,1)}, bf16[128,1536]{1,0:T(8,128)(2,1)}, u32[]{:S(2)}, u32[]{:S(2)}) collective-permute-start(bf16[128,1536]{1,0:T(8,128)(2,1)} %collective-permute-done.6), channel_id=1, source_target_pairs={{0,2},{2,4},{4,6},{6,8},{8,10},{10,12},{12,14},{14,16},{16,18},{18... | collective-permute-start | bytes 1179656 | tf_op jit(solution)/shard_map/ppermute | solution.py:15
  218.7 10.0 %collective-permute-start.9 = (bf16[128,1536]{1,0:T(8,128)(2,1)S(1)}, bf16[128,1536]{1,0:T(8,128)(2,1)}, u32[]{:S(2)}, u32[]{:S(2)}) collective-permute-start(bf16[128,1536]{1,0:T(8,128)(2,1)S(1)} %collective-permute-done.7), channel_id=1, source_target_pairs={{0,2},{2,4},{4,6},{6,8},{8,10},{10,12},{12,14},{14,16},{16,18},{18... | collective-permute-start | bytes 1179656 | tf_op jit(solution)/shard_map/ppermute | solution.py:15
  223.2 58.3 %copy-start.27 = (pred[128,128]{0,1:T(8,128)(4,1)}, pred[128,128]{0,1:T(8,128)(4,1)S(1)}, u32[]{:S(2)}) copy-start(pred[128,128]{0,1:T(8,128)(4,1)S(1)} %get-tuple-element.76) | copy-start | bytes 49156
  226.6 16.7 %collective-permute-start.10 = (bf16[128,1536]{1,0:T(8,128)(2,1)}, bf16[128,1536]{1,0:T(8,128)(2,1)}, u32[]{:S(2)}, u32[]{:S(2)}) collective-permute-start(bf16[128,1536]{1,0:T(8,128)(2,1)} %collective-permute-done.8), channel_id=1, source_target_pairs={{0,2},{2,4},{4,6},{6,8},{8,10},{10,12},{12,14},{14,16},{16,18},{18... | collective-permute-start | bytes 1179656 | tf_op jit(solution)/shard_map/ppermute | solution.py:15
  228.7 16.9 %collective-permute-start.11 = (bf16[128,1536]{1,0:T(8,128)(2,1)}, bf16[128,1536]{1,0:T(8,128)(2,1)}, u32[]{:S(2)}, u32[]{:S(2)}) collective-permute-start(bf16[128,1536]{1,0:T(8,128)(2,1)} %collective-permute-done.9), channel_id=1, source_target_pairs={{0,2},{2,4},{4,6},{6,8},{8,10},{10,12},{12,14},{14,16},{16,18},{18... | collective-permute-start | bytes 1179656 | tf_op jit(solution)/shard_map/ppermute | solution.py:15
  243.3 15.8 %collective-permute-start.12 = (bf16[128,1536]{1,0:T(8,128)(2,1)}, bf16[128,1536]{1,0:T(8,128)(2,1)}, u32[]{:S(2)}, u32[]{:S(2)}) collective-permute-start(bf16[128,1536]{1,0:T(8,128)(2,1)} %collective-permute-done.10), channel_id=1, source_target_pairs={{0,2},{2,4},{4,6},{6,8},{8,10},{10,12},{12,14},{14,16},{16,18},{18... | collective-permute-start | bytes 1179656 | tf_op jit(solution)/shard_map/ppermute | solution.py:15
  245.6 18.2 %collective-permute-start.13 = (bf16[128,1536]{1,0:T(8,128)(2,1)}, bf16[128,1536]{1,0:T(8,128)(2,1)}, u32[]{:S(2)}, u32[]{:S(2)}) collective-permute-start(bf16[128,1536]{1,0:T(8,128)(2,1)} %collective-permute-done.11), channel_id=1, source_target_pairs={{0,2},{2,4},{4,6},{6,8},{8,10},{10,12},{12,14},{14,16},{16,18},{18... | collective-permute-start | bytes 1179656 | tf_op jit(solution)/shard_map/ppermute | solution.py:15
  259.1 18.3 %collective-permute-start.14 = (bf16[128,1536]{1,0:T(8,128)(2,1)}, bf16[128,1536]{1,0:T(8,128)(2,1)S(1)}, u32[]{:S(2)}, u32[]{:S(2)}) collective-permute-start(bf16[128,1536]{1,0:T(8,128)(2,1)} %collective-permute-done.12), channel_id=1, source_target_pairs={{0,2},{2,4},{4,6},{6,8},{8,10},{10,12},{12,14},{14,16},{16,18},{18... | collective-permute-start | bytes 1179656 | tf_op jit(solution)/shard_map/ppermute | solution.py:15
  263.8 13.8 %collective-permute-start.15 = (bf16[128,1536]{1,0:T(8,128)(2,1)}, bf16[128,1536]{1,0:T(8,128)(2,1)}, u32[]{:S(2)}, u32[]{:S(2)}) collective-permute-start(bf16[128,1536]{1,0:T(8,128)(2,1)} %collective-permute-done.13), channel_id=1, source_target_pairs={{0,2},{2,4},{4,6},{6,8},{8,10},{10,12},{12,14},{14,16},{16,18},{18... | collective-permute-start | bytes 1179656 | tf_op jit(solution)/shard_map/ppermute | solution.py:15
  305.2 21.2 %copy-start.7 = (pred[128,2048]{1,0:T(8,128)(4,1)S(1)}, pred[128,2048]{1,0:T(8,128)(4,1)}, u32[]{:S(2)}) copy-start(pred[128,2048]{1,0:T(8,128)(4,1)} %compare_and_fusion) | copy-start | bytes 786436
  310.0 16.5 %copy-start.46 = (f32[16,128]{1,0:T(8,128)}, f32[16,128]{1,0:T(8,128)S(1)}, u32[]{:S(2)}) copy-start(f32[16,128]{1,0:T(8,128)S(1)} %get-tuple-element.62) | copy-start | bytes 24580
  326.4 10.6 %copy-start.8 = (f32[16,128,128]{1,2,0:T(8,128)S(1)}, f32[16,128,128]{1,2,0:T(8,128)}, u32[]{:S(2)}) copy-start(f32[16,128,128]{1,2,0:T(8,128)} %get-tuple-element.79) | copy-start | bytes 3145732
  326.4 10.6 %copy-start.28 = (pred[128,128]{0,1:T(8,128)(4,1)S(1)}, pred[128,128]{0,1:T(8,128)(4,1)}, u32[]{:S(2)}) copy-start(pred[128,128]{0,1:T(8,128)(4,1)} %copy-done.27) | copy-start | bytes 49156
  326.5 10.6 %copy-start.47 = (f32[16,128]{1,0:T(8,128)S(1)}, f32[16,128]{1,0:T(8,128)}, u32[]{:S(2)}) copy-start(f32[16,128]{1,0:T(8,128)} %get-tuple-element.53) | copy-start | bytes 24580
  326.5 10.8 %copy-start.6 = (f32[16,128,128]{1,2,0:T(8,128)S(1)}, f32[16,128,128]{1,2,0:T(8,128)}, u32[]{:S(2)}) copy-start(f32[16,128,128]{1,2,0:T(8,128)} %get-tuple-element.81) | copy-start | bytes 3145732
  326.5 11.0 %copy-start.5 = (f32[16,128,128]{1,2,0:T(8,128)S(1)}, f32[16,128,128]{1,2,0:T(8,128)}, u32[]{:S(2)}) copy-start(f32[16,128,128]{1,2,0:T(8,128)} %get-tuple-element.83) | copy-start | bytes 3145732
  326.5 11.0 %copy-start.33 = (f32[16,128]{1,0:T(8,128)S(1)}, f32[16,128]{1,0:T(8,128)}, u32[]{:S(2)}) copy-start(f32[16,128]{1,0:T(8,128)} %get-tuple-element.55) | copy-start | bytes 24580
  326.5 11.3 %copy-start.4 = (f32[16,128,128]{1,2,0:T(8,128)S(1)}, f32[16,128,128]{1,2,0:T(8,128)}, u32[]{:S(2)}) copy-start(f32[16,128,128]{1,2,0:T(8,128)} %get-tuple-element.85) | copy-start | bytes 3145732
  326.5 11.3 %copy-start.34 = (f32[16,128]{1,0:T(8,128)S(1)}, f32[16,128]{1,0:T(8,128)}, u32[]{:S(2)}) copy-start(f32[16,128]{1,0:T(8,128)} %get-tuple-element.56) | copy-start | bytes 24580
  326.5 11.5 %copy-start.3 = (f32[16,128,128]{1,2,0:T(8,128)S(1)}, f32[16,128,128]{1,2,0:T(8,128)}, u32[]{:S(2)}) copy-start(f32[16,128,128]{1,2,0:T(8,128)} %get-tuple-element.87) | copy-start | bytes 3145732
  326.5 11.5 %copy-start.35 = (f32[16,128]{1,0:T(8,128)S(1)}, f32[16,128]{1,0:T(8,128)}, u32[]{:S(2)}) copy-start(f32[16,128]{1,0:T(8,128)} %get-tuple-element.57) | copy-start | bytes 24580
  326.5 11.7 %copy-start.2 = (f32[16,128,128]{1,2,0:T(8,128)S(1)}, f32[16,128,128]{1,2,0:T(8,128)}, u32[]{:S(2)}) copy-start(f32[16,128,128]{1,2,0:T(8,128)} %get-tuple-element.89) | copy-start | bytes 3145732
  326.5 11.7 %copy-start.22 = (pred[128,128]{0,1:T(8,128)(4,1)S(1)}, pred[128,128]{0,1:T(8,128)(4,1)}, u32[]{:S(2)}) copy-start(pred[128,128]{0,1:T(8,128)(4,1)} %copy-done.21) | copy-start | bytes 49156
  326.6 11.7 %copy-start.36 = (f32[16,128]{1,0:T(8,128)S(1)}, f32[16,128]{1,0:T(8,128)}, u32[]{:S(2)}) copy-start(f32[16,128]{1,0:T(8,128)} %get-tuple-element.58) | copy-start | bytes 24580
  326.6 11.9 %copy-start.1 = (f32[16,128,128]{1,2,0:T(8,128)S(1)}, f32[16,128,128]{1,2,0:T(8,128)}, u32[]{:S(2)}) copy-start(f32[16,128,128]{1,2,0:T(8,128)} %get-tuple-element.91) | copy-start | bytes 3145732
  326.6 11.9 %copy-start.24 = (pred[128,128]{0,1:T(8,128)(4,1)S(1)}, pred[128,128]{0,1:T(8,128)(4,1)}, u32[]{:S(2)}) copy-start(pred[128,128]{0,1:T(8,128)(4,1)} %copy-done.23) | copy-start | bytes 49156
  326.6 11.9 %copy-start.37 = (f32[16,128]{1,0:T(8,128)S(1)}, f32[16,128]{1,0:T(8,128)}, u32[]{:S(2)}) copy-start(f32[16,128]{1,0:T(8,128)} %get-tuple-element.59) | copy-start | bytes 24580
  326.6 12.1 %copy-start.38 = (f32[16,128]{1,0:T(8,128)S(1)}, f32[16,128]{1,0:T(8,128)}, u32[]{:S(2)}) copy-start(f32[16,128]{1,0:T(8,128)} %get-tuple-element.60) | copy-start | bytes 24580
  326.6 12.3 %copy-start.26 = (pred[128,128]{0,1:T(8,128)(4,1)S(1)}, pred[128,128]{0,1:T(8,128)(4,1)}, u32[]{:S(2)}) copy-start(pred[128,128]{0,1:T(8,128)(4,1)} %copy-done.25) | copy-start | bytes 49156
  326.6 12.3 %copy-start.39 = (f32[16,128]{1,0:T(8,128)S(1)}, f32[16,128]{1,0:T(8,128)}, u32[]{:S(2)}) copy-start(f32[16,128]{1,0:T(8,128)} %get-tuple-element.61) | copy-start | bytes 24580
  326.6 12.5 %copy-start.44 = (f32[16,128]{1,0:T(8,128)S(1)}, f32[16,128]{1,0:T(8,128)}, u32[]{:S(2)}) copy-start(f32[16,128]{1,0:T(8,128)} %get-tuple-element.68) | copy-start | bytes 24580
  326.6 13.4 %copy-start.29 = (f32[16,128]{1,0:T(8,128)S(1)}, f32[16,128]{1,0:T(8,128)}, u32[]{:S(2)}) copy-start(f32[16,128]{1,0:T(8,128)} %get-tuple-element.92) | copy-start | bytes 24580
  326.6 13.4 %copy-start.30 = (f32[16,128]{1,0:T(8,128)S(1)}, f32[16,128]{1,0:T(8,128)}, u32[]{:S(2)}) copy-start(f32[16,128]{1,0:T(8,128)} %get-tuple-element.88) | copy-start | bytes 24580
  326.7 13.4 %copy-start.32 = (f32[16,128]{1,0:T(8,128)S(1)}, f32[16,128]{1,0:T(8,128)}, u32[]{:S(2)}) copy-start(f32[16,128]{1,0:T(8,128)} %get-tuple-element.96) | copy-start | bytes 24580
  326.7 13.4 %copy-start.40 = (f32[16,128]{1,0:T(8,128)S(1)}, f32[16,128]{1,0:T(8,128)}, u32[]{:S(2)}) copy-start(f32[16,128]{1,0:T(8,128)} %get-tuple-element.84) | copy-start | bytes 24580
  326.7 13.4 %copy-start.41 = (f32[16,128]{1,0:T(8,128)S(1)}, f32[16,128]{1,0:T(8,128)}, u32[]{:S(2)}) copy-start(f32[16,128]{1,0:T(8,128)} %get-tuple-element.82) | copy-start | bytes 24580
  326.7 13.4 %copy-start.42 = (f32[16,128]{1,0:T(8,128)S(1)}, f32[16,128]{1,0:T(8,128)}, u32[]{:S(2)}) copy-start(f32[16,128]{1,0:T(8,128)} %get-tuple-element.80) | copy-start | bytes 24580
  326.7 13.4 %copy-start.43 = (f32[16,128]{1,0:T(8,128)S(1)}, f32[16,128]{1,0:T(8,128)}, u32[]{:S(2)}) copy-start(f32[16,128]{1,0:T(8,128)} %get-tuple-element.78) | copy-start | bytes 24580
  326.7 13.4 %copy-start.45 = (f32[16,128]{1,0:T(8,128)S(1)}, f32[16,128]{1,0:T(8,128)}, u32[]{:S(2)}) copy-start(f32[16,128]{1,0:T(8,128)} %fusion.1) | copy-start | bytes 24580
  326.7 14.2 %copy-start.31 = (bf16[8,16,96]{2,1,0:T(8,128)(2,1)S(1)}, bf16[8,16,96]{2,1,0:T(8,128)(2,1)}, u32[]{:S(2)}) copy-start(bf16[8,16,96]{2,1,0:T(8,128)(2,1)} %reshape.1639) | copy-start | bytes 73732
  326.7 15.3 %copy-start.9 = (bf16[128,1536]{0,1:T(8,128)(2,1)S(1)}, bf16[128,1536]{0,1:T(8,128)(2,1)}, u32[]{:S(2)}) copy-start(bf16[128,1536]{0,1:T(8,128)(2,1)} %copy.96) | copy-start | bytes 1179652
  326.7 15.6 %copy-start.10 = (bf16[128,1536]{0,1:T(8,128)(2,1)S(1)}, bf16[128,1536]{0,1:T(8,128)(2,1)}, u32[]{:S(2)}) copy-start(bf16[128,1536]{0,1:T(8,128)(2,1)} %copy.99) | copy-start | bytes 1179652
  (11 other events, 61.9 us)
Sparse Core Ops, SparseCore 0:
  28.8 288.1 all-gather.1
  347.8 22.1 reduce-scatter.1
